TPU v7x, 32 devices: a whole 2x2x4 slice. The times are simulated.
32 devices in a mesh: shard: 4 (over x, core), ctx: 4 (over z), tp: 2 (over y).
Axes of the slice: x: 2, y: 2, z: 4, core: 2. Of those that a mesh axis runs over, the one named last changes fastest.
Arguments:
- hidden_in: bfloat16 [4096, 2048], P(('shard', 'ctx')), may hold values from -6 to 6
- gain_attn: bfloat16 [2048], P(('shard', 'ctx')), may hold values from 0.5 to 1.5
- w_qkv: bfloat16 [3, 2048, 2048], P(None, ('shard', 'ctx'), 'tp'), may hold values from -1 to 1
- w_out: bfloat16 [2048, 2048], P('tp', ('shard', 'ctx')), may hold values from -0.5 to 0.5
- gain_mlp: bfloat16 [2048], P(('shard', 'ctx')), may hold values from 0.5 to 1.5
- w_gate_up: bfloat16 [2, 2048, 8192], P(None, ('shard', 'ctx'), 'tp'), may hold values from -0.125 to 0.125
- w_down: bfloat16 [8192, 2048], P('tp', ('shard', 'ctx')), may hold values from -0.0625 to 0.0625
- segments: int32 [4, 1024], P('shard'), may hold values from 0 to 3, never falling along the last dimension, each value on 1 to 512 neighbouring positions
- cotangent: bfloat16 [4096, 2048], P(('shard', 'ctx')), may hold values from -6 to 6
Outputs:
- block_out: bfloat16 [4096, 2048], P(('shard', 'ctx'))
- grad_input: float32 [4096, 2048], P(('shard', 'ctx'))
- grad_gain_attn: float32 [2048], P(('shard', 'ctx'))
- grad_w_qkv: float32 [3, 2048, 2048], P(None, ('shard', 'ctx'), 'tp')
- grad_w_out: float32 [2048, 2048], P('tp', ('shard', 'ctx'))
- grad_gain_mlp: float32 [2048], P(('shard', 'ctx'))
- grad_w_gate_up: float32 [2, 2048, 8192], P(None, ('shard', 'ctx'), 'tp')
- grad_w_down: float32 [8192, 2048], P('tp', ('shard', 'ctx'))
Inputs may be any that keep to these rules, and one draw needn't show every extreme that they name: `segments`: each row holds one group's 1024 segment numbers; they never fall, and each segment covers 1 to 512 positions, one exactly 512.
All inputs are finite; a program needn't handle non-finite values.
Results may differ from a plain program's by a relative error of at most 0.025.
Values may be sent and summed in bfloat16 or wider, within the bound.
No kernel may reach another device: no remote copies, remote signals or barrier semaphores. Data moves between devices by JAX's collectives and lax.ppermute only.
A program may use at most 256 MiB of HBM per device.

v0:
```python
import jax
import jax.numpy as jnp
from jax import lax
from jax.sharding import PartitionSpec as P

HD = 64
EPSILON = 1e-05
ROPE_BASE = 130000.0
MASKED = -1e30


def contract(form, left_in, right_in):
    return jnp.einsum(form, left_in, right_in, preferred_element_type=jnp.float32)


def positions_of(seg_row):
    length_all = seg_row.shape[0]
    index_all = jnp.arange(length_all, dtype=jnp.int32)
    starts = jnp.concatenate([jnp.ones((1,), dtype=jnp.bool_), seg_row[1:] != seg_row[:-1]])
    first_index = lax.cummax(jnp.where(starts, index_all, jnp.zeros_like(index_all)), axis=0)
    return index_all - first_index


def rope_tables(positions, head_size):
    half_size = head_size // 2
    frequency = ROPE_BASE ** (-(jnp.arange(half_size, dtype=jnp.float32) * (2.0 / head_size)))
    angles = positions.astype(jnp.float32)[:, None] * frequency[None, :]
    return (jnp.cos(angles), jnp.sin(angles))


def rotate_heads(values_in, cosine_table, sine_table, head_size):
    rows_count = values_in.shape[0]
    shaped = values_in.reshape(rows_count, -1, head_size)
    half_size = head_size // 2
    first_half = shaped[..., :half_size]
    second_half = shaped[..., half_size:]
    cosine_rows = cosine_table[:, None, :]
    sine_rows = sine_table[:, None, :]
    turned = jnp.concatenate(
        [
            first_half * cosine_rows - second_half * sine_rows,
            second_half * cosine_rows + first_half * sine_rows,
        ],
        -1,
    )
    return turned.reshape(rows_count, -1)


def block_layout(array_in, block_rows):
    blocks_count = array_in.shape[0] // block_rows
    return array_in.reshape((blocks_count, block_rows) + array_in.shape[1:])


def with_previous(blocks, fill_value):
    earlier = jnp.concatenate([jnp.full_like(blocks[:1], fill_value), blocks[:-1]], 0)
    return jnp.concatenate([earlier, blocks], 1)


def block_masks(seg_row, block_rows):
    index_all = jnp.arange(seg_row.shape[0], dtype=jnp.int32)
    seg_query = block_layout(seg_row, block_rows)
    index_query = block_layout(index_all, block_rows)
    return (seg_query, index_query, with_previous(seg_query, -1), with_previous(index_query, 0))


def heads_view(array_in, head_size):
    return array_in.reshape(array_in.shape[0], -1, head_size)


def block_scores(
    query_blk, key_blk, seg_query_blk, index_query_blk, seg_key_blk, index_key_blk, head_size
):
    allowed = (seg_key_blk[None, :] == seg_query_blk[:, None]) & (
        index_key_blk[None, :] <= index_query_blk[:, None]
    )
    scores = contract("qhd,khd->hqk", query_blk, key_blk) * head_size ** (-0.5)
    return jnp.where(allowed[None], scores, MASKED)


def attention_forward(queries, keys_rot, value_vecs, seg_row, head_size):
    group_rows = queries.shape[0]
    block_rows = min(512, group_rows)
    query_blocks = block_layout(heads_view(queries, head_size), block_rows)
    key_blocks = with_previous(block_layout(heads_view(keys_rot, head_size), block_rows), 0)
    value_blocks = with_previous(block_layout(heads_view(value_vecs, head_size), block_rows), 0)
    seg_query, index_query, seg_keys, index_keys = block_masks(seg_row, block_rows)

    def one_block(block_items):
        query_blk, key_blk, value_blk, seg_qb, index_qb, seg_kb, index_kb = block_items
        scores = block_scores(query_blk, key_blk, seg_qb, index_qb, seg_kb, index_kb, head_size)
        row_max = jnp.max(scores, -1, keepdims=True)
        log_total = row_max + jnp.log(jnp.sum(jnp.exp(scores - row_max), -1, keepdims=True))
        weights_low = jnp.exp(scores - log_total).astype(jnp.bfloat16)
        block_result = contract("hqk,khd->qhd", weights_low, value_blk)
        return (block_result.astype(jnp.bfloat16).reshape(block_rows, -1), log_total[..., 0])

    result_blocks, log_blocks = lax.map(
        one_block,
        (query_blocks, key_blocks, value_blocks, seg_query, index_query, seg_keys, index_keys),
    )
    return (result_blocks.reshape(group_rows, -1), log_blocks)


def attention_backward(
    queries, keys_rot, value_vecs, attn, grad_attn, log_blocks, seg_row, head_size
):
    group_rows = queries.shape[0]
    block_rows = min(512, group_rows)
    score_scale = head_size ** (-0.5)
    query_blocks = block_layout(heads_view(queries, head_size), block_rows)
    key_blocks = with_previous(block_layout(heads_view(keys_rot, head_size), block_rows), 0)
    value_blocks = with_previous(block_layout(heads_view(value_vecs, head_size), block_rows), 0)
    attn_blocks = block_layout(heads_view(attn, head_size), block_rows)
    grad_blocks = block_layout(heads_view(grad_attn, head_size), block_rows)
    seg_query, index_query, seg_keys, index_keys = block_masks(seg_row, block_rows)

    def one_block(block_items):
        (
            query_blk,
            key_blk,
            value_blk,
            attn_blk,
            grad_blk,
            log_blk,
            seg_qb,
            index_qb,
            seg_kb,
            index_kb,
        ) = block_items
        scores = block_scores(query_blk, key_blk, seg_qb, index_qb, seg_kb, index_kb, head_size)
        probs = jnp.exp(scores - log_blk[..., None])
        probs_low = probs.astype(jnp.bfloat16)
        grad_value_blk = contract("hqk,qhd->khd", probs_low, grad_blk)
        grad_probs = contract("qhd,khd->hqk", grad_blk, value_blk)
        diag = jnp.sum(grad_blk.astype(jnp.float32) * attn_blk.astype(jnp.float32), -1).T
        grad_scores = (probs * (grad_probs - diag[..., None])).astype(jnp.bfloat16)
        grad_query_blk = contract("hqk,khd->qhd", grad_scores, key_blk) * score_scale
        grad_key_blk = contract("hqk,qhd->khd", grad_scores, query_blk) * score_scale
        return (grad_query_blk, grad_key_blk, grad_value_blk)

    grad_query_b, grad_key_b, grad_value_b = lax.map(
        one_block,
        (
            query_blocks,
            key_blocks,
            value_blocks,
            attn_blocks,
            grad_blocks,
            log_blocks,
            seg_query,
            index_query,
            seg_keys,
            index_keys,
        ),
    )

    def fold_pairs(pairs):
        earlier = pairs[:, :block_rows]
        current = pairs[:, block_rows:]
        shifted = jnp.concatenate([earlier[1:], jnp.zeros_like(earlier[:1])], 0)
        return (current + shifted).reshape(group_rows, -1).astype(jnp.bfloat16)

    return (
        grad_query_b.reshape(group_rows, -1).astype(jnp.bfloat16),
        fold_pairs(grad_key_b),
        fold_pairs(grad_value_b),
    )


def on_device(hidden_in, gain_attn, w_qkv, w_out, gain_mlp, w_gate_up, w_down, segments, cotangent):
    token_rows = hidden_in.shape[0]
    seg_row = segments[0]
    positions = lax.dynamic_slice_in_dim(
        positions_of(seg_row), lax.axis_index("ctx") * token_rows, token_rows
    )
    cosine_table, sine_table = rope_tables(positions, HD)
    gathered = (
        lax.all_gather(gain_attn, ("shard", "ctx"), axis=0, tiled=True),
        lax.all_gather(w_qkv, ("shard", "ctx"), axis=1, tiled=True),
        lax.all_gather(w_out, ("shard", "ctx"), axis=1, tiled=True),
        lax.all_gather(gain_mlp, ("shard", "ctx"), axis=0, tiled=True),
        lax.all_gather(w_gate_up, ("shard", "ctx"), axis=1, tiled=True),
        lax.all_gather(w_down, ("shard", "ctx"), axis=1, tiled=True),
    )
    gain_full_one, qkv_full, out_full, gain_full_two, gate_up_full, down_full = gathered
    resid_in = hidden_in.astype(jnp.float32)
    scale_one = lax.rsqrt(jnp.mean(resid_in * resid_in, -1, keepdims=True) + EPSILON)
    gain_one = gain_full_one.astype(jnp.float32)
    normed_one = (resid_in * scale_one * gain_one).astype(jnp.bfloat16)
    projected = contract("td,jdc->jtc", normed_one, qkv_full)
    queries = rotate_heads(projected[0], cosine_table, sine_table, HD).astype(jnp.bfloat16)
    keys_rot = rotate_heads(projected[1], cosine_table, sine_table, HD).astype(jnp.bfloat16)
    value_vecs = projected[2].astype(jnp.bfloat16)
    query_heads, key_heads, value_heads = (
        lax.all_to_all(queries, "ctx", split_axis=1, concat_axis=0, tiled=True),
        lax.all_to_all(keys_rot, "ctx", split_axis=1, concat_axis=0, tiled=True),
        lax.all_to_all(value_vecs, "ctx", split_axis=1, concat_axis=0, tiled=True),
    )
    attn_heads, log_blocks = attention_forward(query_heads, key_heads, value_heads, seg_row, HD)
    attn_tokens = lax.all_to_all(attn_heads, "ctx", split_axis=0, concat_axis=1, tiled=True)
    attn_terms = jnp.dot(attn_tokens, out_full, preferred_element_type=jnp.float32)
    gain_two = gain_full_two.astype(jnp.float32)
    resid_mid = resid_in + lax.psum(attn_terms.astype(jnp.bfloat16), "tp").astype(jnp.float32)
    scale_two = lax.rsqrt(jnp.mean(resid_mid * resid_mid, -1, keepdims=True) + EPSILON)
    normed_two = (resid_mid * scale_two * gain_two).astype(jnp.bfloat16)
    gate_up = contract("td,jdf->jtf", normed_two, gate_up_full)
    gate_proj = gate_up[0]
    up_proj = gate_up[1]
    sigmoid_gate = jax.nn.sigmoid(gate_proj)
    activated = (gate_proj * sigmoid_gate * up_proj).astype(jnp.bfloat16)
    mlp_terms = jnp.dot(activated, down_full, preferred_element_type=jnp.float32)
    block_out = (
        resid_mid + lax.psum(mlp_terms.astype(jnp.bfloat16), "tp").astype(jnp.float32)
    ).astype(jnp.bfloat16)
    again = (
        lax.all_gather(w_qkv, ("shard", "ctx"), axis=1, tiled=True),
        lax.all_gather(w_out, ("shard", "ctx"), axis=1, tiled=True),
        lax.all_gather(w_gate_up, ("shard", "ctx"), axis=1, tiled=True),
        lax.all_gather(w_down, ("shard", "ctx"), axis=1, tiled=True),
    )
    qkv_back, out_back, gate_up_back, down_back = again
    grad_act = contract("td,fd->tf", cotangent, down_back)
    grad_w_down = contract("tf,td->fd", activated, cotangent)
    grad_gate = grad_act * up_proj * sigmoid_gate * (1.0 + gate_proj * (1.0 - sigmoid_gate))
    grad_up = grad_act * gate_proj * sigmoid_gate
    grad_pair = jnp.stack([grad_gate, grad_up]).astype(jnp.bfloat16)
    grad_w_gate_up = contract("td,jtf->jdf", normed_two, grad_pair)
    terms_two = contract("jtf,jdf->td", grad_pair, gate_up_back)
    grad_normed_two = lax.psum(terms_two.astype(jnp.bfloat16), "tp").astype(jnp.float32)
    cot_rows = cotangent.astype(jnp.float32)
    grad_gain_mlp = jnp.sum(grad_normed_two * resid_mid * scale_two, 0)
    scaled_two = grad_normed_two * gain_two
    grad_mid = (
        cot_rows
        + scale_two * scaled_two
        - resid_mid * scale_two**3 * jnp.mean(scaled_two * resid_mid, -1, keepdims=True)
    )
    grad_mid_low = grad_mid.astype(jnp.bfloat16)
    grad_w_out = contract("tc,td->cd", attn_tokens, grad_mid_low)
    grad_attn_tokens = contract("td,cd->tc", grad_mid_low, out_back).astype(jnp.bfloat16)
    grad_attn_heads = lax.all_to_all(
        grad_attn_tokens, "ctx", split_axis=1, concat_axis=0, tiled=True
    )
    grad_query_heads, grad_key_heads, grad_value_heads = attention_backward(
        query_heads, key_heads, value_heads, attn_heads, grad_attn_heads, log_blocks, seg_row, HD
    )
    grad_queries, grad_keys, grad_values = (
        lax.all_to_all(grad_query_heads, "ctx", split_axis=0, concat_axis=1, tiled=True),
        lax.all_to_all(grad_key_heads, "ctx", split_axis=0, concat_axis=1, tiled=True),
        lax.all_to_all(grad_value_heads, "ctx", split_axis=0, concat_axis=1, tiled=True),
    )
    pre_query = rotate_heads(
        grad_queries.astype(jnp.float32), cosine_table, -sine_table, HD
    ).astype(jnp.bfloat16)
    pre_key = rotate_heads(grad_keys.astype(jnp.float32), cosine_table, -sine_table, HD).astype(
        jnp.bfloat16
    )
    grad_proj = jnp.stack([pre_query, pre_key, grad_values])
    grad_w_qkv = contract("td,jtc->jdc", normed_one, grad_proj)
    terms_one = contract("jtc,jdc->td", grad_proj, qkv_back)
    grad_normed_one = lax.psum(terms_one.astype(jnp.bfloat16), "tp").astype(jnp.float32)
    grad_gain_attn = jnp.sum(grad_normed_one * resid_in * scale_one, 0)
    scaled_one = grad_normed_one * gain_one
    grad_input = (
        grad_mid
        + scale_one * scaled_one
        - resid_in * scale_one**3 * jnp.mean(scaled_one * resid_in, -1, keepdims=True)
    )
    owned = (
        lax.psum_scatter(
            grad_gain_attn.astype(jnp.bfloat16), ("shard", "ctx"), scatter_dimension=0, tiled=True
        ).astype(jnp.float32),
        lax.psum_scatter(
            grad_w_qkv.astype(jnp.bfloat16), ("shard", "ctx"), scatter_dimension=1, tiled=True
        ).astype(jnp.float32),
        lax.psum_scatter(
            grad_w_out.astype(jnp.bfloat16), ("shard", "ctx"), scatter_dimension=1, tiled=True
        ).astype(jnp.float32),
        lax.psum_scatter(
            grad_gain_mlp.astype(jnp.bfloat16), ("shard", "ctx"), scatter_dimension=0, tiled=True
        ).astype(jnp.float32),
        lax.psum_scatter(
            grad_w_gate_up.astype(jnp.bfloat16), ("shard", "ctx"), scatter_dimension=1, tiled=True
        ).astype(jnp.float32),
        lax.psum_scatter(
            grad_w_down.astype(jnp.bfloat16), ("shard", "ctx"), scatter_dimension=1, tiled=True
        ).astype(jnp.float32),
    )
    return (block_out, grad_input, owned[0], owned[1], owned[2], owned[3], owned[4], owned[5])


def solution(mesh):
    placed = (
        P(("shard", "ctx"), None),
        P(("shard", "ctx")),
        P(None, ("shard", "ctx"), "tp"),
        P("tp", ("shard", "ctx")),
        P(("shard", "ctx")),
        P(None, ("shard", "ctx"), "tp"),
        P("tp", ("shard", "ctx")),
        P("shard", None),
        P(("shard", "ctx"), None),
    )
    return jax.shard_map(
        on_device,
        mesh=mesh,
        in_specs=placed,
        out_specs=(
            P(("shard", "ctx"), None),
            P(("shard", "ctx"), None),
            P(("shard", "ctx")),
            P(None, ("shard", "ctx"), "tp"),
            P("tp", ("shard", "ctx")),
            P(("shard", "ctx")),
            P(None, ("shard", "ctx"), "tp"),
            P("tp", ("shard", "ctx")),
        ),
        check_vma=False,
    )
```

profile of v0, /device:TPU:0, one launch (start us, length us, event | category | flops | bytes accessed | tf_op | source)
XLA Modules:
  0.0 1597.4 jit_solution(17848206042767868809)
XLA Ops:
  8.7 35.0 %all-gather = bf16[16,1,128]{2,1,0:T(2,128)(2,1)S(1)} all-gather(bf16[1,1,128]{2,1,0:T(2,128)(2,1)} %bitcast.306), channel_id=1, replica_groups=mesh['shard'=4,'ctx'=4,'tp'=2] {'shard','ctx'}, dimensions={0}, use_global_device_ids=true | all-gather | bytes 4352 | tf_op jit(solution)/shard_map/all_gather | solution.py:178
  46.6 66.9 %all-gather.7.cloned.1.call-done = bf16[3,2048,1024]{2,1,0:T(8,128)(2,1)} async-done(((bf16[3,128,1024]{2,1,0:T(8,128)(2,1)}), bf16[3,2048,1024]{2,1,0:T(8,128)(2,1)}) %all-gather.7.cloned.1.call-update) | async-done | bytes 12582928 | tf_op jit(solution)/shard_map/all_gather | solution.py:179
  113.5 6.5 convolution_bitcast_fusion.3
  122.8 4.1 all-to-all-start
  127.7 2.7 fusion.93
  134.2 13.5 all-to-all-done
  147.8 3.5 all-to-all-start.2
  152.1 26.5 %all-to-all-done.2 = bf16[256,4,256]{0,2,1:T(8,128)(2,1)S(1)} async-done(((bf16[256,4,256]{0,2,1:T(8,128)(2,1)}), bf16[256,4,256]{0,2,1:T(8,128)(2,1)S(1)}, u32[]{:S(2)}, u32[]{:S(2)}) %all-to-all-start.2) | async-done | bytes 524320 | tf_op jit(solution)/shard_map/all_to_all | solution.py:196
  178.6 3.5 all-to-all-start.1
  194.7 2.5 all-to-all-done.1
  198.0 2.5 fusion.76
  200.5 14.2 while.26
  202.7 2.4 exponential_reduce_fusion.2
  205.2 2.4 fusion.130
  209.8 2.4 exponential_reduce_fusion.2
  212.3 2.3 fusion.130
  215.7 18.5 %all_to_all.107 = bf16[4,256,256]{2,1,0:T(8,128)(2,1)} all-to-all(bf16[4,256,256]{2,1,0:T(8,128)(2,1)} %bitcast.284), channel_id=1, replica_groups=mesh['shard'=4,'ctx'=4,'tp'=2] {'ctx'}, dimensions={0} | all-to-all | bytes 1048576 | tf_op jit(solution)/shard_map/all_to_all | solution.py:200
  236.3 4.6 convolution_convert_fusion.3
  242.1 28.8 %all-gather.1 = bf16[16,1,128]{2,1,0:T(2,128)(2,1)S(1)} all-gather(bf16[1,1,128]{2,1,0:T(2,128)(2,1)S(1)} %bitcast.307), channel_id=1, replica_groups=mesh['shard'=4,'ctx'=4,'tp'=2] {'shard','ctx'}, dimensions={0}, use_global_device_ids=true | all-gather | bytes 4352 | tf_op jit(solution)/shard_map/all_gather | solution.py:181
  270.9 8.4 all-reduce.14.cloned.1.call-done
  281.0 177.7 %all-gather.11.cloned.1.call-done = bf16[2,2048,4096]{2,1,0:T(8,128)(2,1)} async-done(((bf16[2,128,4096]{2,1,0:T(8,128)(2,1)}), bf16[2,2048,4096]{2,1,0:T(8,128)(2,1)}) %all-gather.11.cloned.1.call-update) | async-done | bytes 33554448 | tf_op jit(solution)/shard_map/all_gather | solution.py:182
  458.6 18.2 %convolution_bitcast_fusion = f32[2,256,4096]{2,1,0:T(8,128)} fusion(bf16[2,2048,4096]{2,1,0:T(8,128)(2,1)} %all-gather.11.cloned.1.call-done, bf16[256,2048]{1,0:T(8,128)(2,1)} %all-reduce.14.cloned.1.call-done, bf16[256,2048]{1,0:T(8,128)(2,1)S(1)} %copy-done, f32[2048]{0:T(1024)S(1)} %bitcast.300, f32[256]{0:T(256)S(1)} %get-tuple-element.337), kind=kOutput, calls=%fused_computation.72 | convolution fusion | flops 8593080320 | bytes 44049408 | tf_op jit(solution)/shard_map/td,jdf->jtf/dot_general | solution.py:13
  476.8 113.6 %all-gather.13.cloned.1.call-done = bf16[4096,2048]{1,0:T(8,128)(2,1)} async-done(((bf16[4096,128]{1,0:T(8,128)(2,1)}), bf16[4096,2048]{1,0:T(8,128)(2,1)}) %all-gather.13.cloned.1.call-update) | async-done | bytes 16777232 | tf_op jit(solution)/shard_map/all_gather | solution.py:183
  590.4 13.4 fusion.74
  603.8 16.7 %fusion.52 = bf16[256,2048]{1,0:T(8,128)(2,1)} fusion(bf16[2,2048,4096]{2,1,0:T(8,128)(2,1)} %all-gather.11.cloned.1.call-done, bf16[1,256,4096]{2,1,0:T(8,128)(2,1)} %get-tuple-element.313, bf16[1,256,4096]{2,1,0:T(8,128)(2,1)} %get-tuple-element.312), kind=kOutput, calls=%fused_computation.92 | convolution fusion | flops 8592556032 | bytes 38797312 | tf_op jit(solution)/shard_map/jtf,jdf->td/dot_general | solution.py:13
  620.5 38.4 %all-reduce.16.cloned.1.call-done = bf16[256,2048]{1,0:T(8,128)(2,1)} async-done(((bf16[256,2048]{1,0:T(8,128)(2,1)}), bf16[256,2048]{1,0:T(8,128)(2,1)}) %all-reduce.16.cloned.1.call-update) | async-done | bytes 1048592 | tf_op jit(solution)/shard_map/psum | solution.py:229
  659.0 3.0 fusion.63
  662.0 3.8 convolution_convert_fusion.4
  666.8 4.8 all-to-all-start.4
  671.7 14.3 all-to-all-done.4
  687.2 2.7 reshape_reshape.18
  691.0 24.8 %while.27 = (s32[]{:T(128)}, bf16[2,512,4,64]{1,3,2,0:T(8,128)(2,1)}, f32[2,1024,4,64]{1,3,2,0:T(8,128)}, f32[2,1024,4,64]{1,3,2,0:T(8,128)}, bf16[2,1024,4,64]{...) while((s32[]{:T(128)}, ...), condition=%wide.region_14.15_spmd, body=%wide.region_12.14_spmd.sunk | while | flops 1365637120 | bytes 89220488 | solution.py:141
  693.0 3.3 multiply_convert_fusion.6
  699.6 2.4 fusion.145
  705.4 3.3 multiply_convert_fusion.6
  712.0 2.4 fusion.145
  719.8 3.5 all-to-all-start.7
  724.9 12.4 all-to-all-done.7
  737.3 4.5 all-to-all-start.5
  745.6 2.9 convert_element_type.229
  750.4 5.6 all-to-all-done.5
  756.0 4.1 all-to-all-start.6
  760.2 9.2 convolution_convert_fusion.2
  772.0 2.2 all-to-all-done.6
  777.6 9.0 fusion.53
  788.1 5.0 convolution_convert_fusion.1
  793.1 6.4 copy.113
  800.2 7.9 convert_bitcast_fusion.1
  808.1 27.7 %copy.111 = bf16[3,2048,1024]{2,0,1:T(4,128)(2,1)} copy(bf16[3,2048,1024]{1,2,0:T(8,128)(2,1)} %convert_bitcast_fusion.1) | data formatting | bytes 25165824
  835.8 15.8 copy.119
  851.7 10.1 convolution_convert_fusion
  861.8 21.6 %copy.117 = bf16[4096,2048]{0,1:T(8,128)(2,1)} copy(bf16[4096,2048]{1,0:T(8,128)(2,1)} %convolution_convert_fusion) | data formatting | bytes 33554432
  883.7 16.4 %convert_bitcast_fusion = bf16[2,2048,4096]{1,2,0:T(8,128)(2,1)} fusion(bf16[1,256,4096]{2,1,0:T(8,128)(2,1)} %get-tuple-element.313, bf16[1,256,4096]{2,1,0:T(8,128)(2,1)} %get-tuple-element.312, bf16[256,2048]{1,0:T(8,128)(2,1)S(1)} %copy-done.3, bf16[256,2048]{1,0:T(8,128)(2,1)S(1)} %copy-done, f32[2048]{0:T(1024)S(1)} %bitcast.304, ...), kind=kOutput, calls=%fused_computation.69 | convolution fusion | flops 8611954688 | bytes 39855104 | tf_op jit(solution)/shard_map/td,jtf->jdf/dot_general | solution.py:13
  900.1 83.3 %copy.115 = bf16[2,2048,4096]{2,0,1:T(2,128)(2,1)} copy(bf16[2,2048,4096]{1,2,0:T(8,128)(2,1)} %convert_bitcast_fusion) | data formatting | bytes 67108864
  983.5 29.6 %copy.120 = bf16[256,8,2,4096]{3,1,2,0:T(8,128)(2,1)} copy(bf16[256,8,2,4096]{3,2,1,0:T(2,128)(2,1)} %bitcast.260) | data formatting | bytes 67108864
  1016.8 33.2 %all-reduce.8 = (bf16[2048]{0:T(1024)(128)(2,1)S(1)}, bf16[2048]{0:T(1024)(128)(2,1)S(1)}) all-reduce(bf16[2048]{0:T(1024)(128)(2,1)S(1)} %get-tuple-element.246, bf16[2048]{0:T(1024)(128)(2,1)S(1)} %copy-done.32), channel_id=2, replica_groups=mesh['shard'=4,'ctx'=4,'tp'=2] {'shard','ctx'}, use_global_device_ids=true, to_apply=%region_18.19.clone | all-reduce | flops 4096 | bytes 16384
  1051.3 5.1 fusion.58
  1058.4 5.2 reduce-scatter.13.cloned.1.call-done
  1063.6 2.7 reshape.424
  1068.6 175.6 %reduce-scatter.19.cloned.1.call-done = bf16[128,4096]{1,0:T(8,128)(2,1)} async-done(((bf16[2048,4096]{1,0:T(8,128)(2,1)}), bf16[128,4096]{1,0:T(8,128)(2,1)}) %reduce-scatter.19.cloned.1.call-update) | async-done | bytes 1048592
  1247.2 330.9 %reduce-scatter.17.cloned.1.call-done = bf16[128,8192]{1,0:T(8,128)(2,1)} async-done(((bf16[2048,8192]{1,0:T(8,128)(2,1)}), bf16[128,8192]{1,0:T(8,128)(2,1)}) %reduce-scatter.17.cloned.1.call-update) | async-done | bytes 2097168
  1578.1 4.5 reshape.428
  1582.6 4.9 copy.116
  1587.5 3.2 copy.105
  (231 shorter events, 83.9 us)
Async XLA Ops:
  7.2 106.4 %copy-start = (bf16[256,2048]{1,0:T(8,128)(2,1)S(1)}, bf16[256,2048]{1,0:T(8,128)(2,1)}, u32[]{:S(2)}) copy-start(bf16[256,2048]{1,0:T(8,128)(2,1)} %param.13) | copy-start | bytes 3145732
  7.2 38.6 %copy-start.29 = (s32[1,1024]{1,0:T(1,128)S(1)}, s32[1,1024]{1,0:T(1,128)}, u32[]{:S(2)}) copy-start(s32[1,1024]{1,0:T(1,128)} %param.20) | copy-start | bytes 12292
  7.2 106.3 %all-gather.7.cloned.1.call-start = ((), (), s32[]{:S(2)}) async-start(), calls=%async_computation.12 | async-start | bytes 13369344 | tf_op jit(solution)/shard_map/all_gather | solution.py:179
  7.9 228.3 %all-gather.9.cloned.1.call-start = ((), (), s32[]{:S(2)}) async-start(), calls=%async_computation.13 | async-start | bytes 4456448 | tf_op jit(solution)/shard_map/all_gather | solution.py:180
  43.7 69.9 %copy-start.24 = (f32[16,1,128]{2,1,0:T(1,128)}, f32[16,1,128]{2,1,0:T(1,128)S(1)}, u32[]{:S(2)}) copy-start(f32[16,1,128]{2,1,0:T(1,128)S(1)} %convert_element_type.257) | copy-start | bytes 24580
  45.8 67.8 %copy-start.30 = (f32[256]{0:T(256)}, f32[256]{0:T(256)S(1)}, u32[]{:S(2)}) copy-start(f32[256]{0:T(256)S(1)} %get-tuple-element.335) | copy-start | bytes 3076
  120.0 1.7 copy-start.1
  122.8 25.0 %all-to-all-start = ((bf16[256,4,256]{0,2,1:T(8,128)(2,1)}), bf16[256,4,256]{0,2,1:T(8,128)(2,1)}, u32[]{:S(2)}, u32[]{:S(2)}) async-start(bf16[256,4,256]{0,2,1:T(8,128)(2,1)} %bitcast.31), calls=%async_computation | async-start | bytes 1048576 | tf_op jit(solution)/shard_map/all_to_all | solution.py:197
  127.7 4.6 copy-start.26
  133.4 17.9 %copy-start.17 = (bf16[256,16,32]{0,2,1:T(8,128)(2,1)S(1)}, bf16[256,16,32]{0,2,1:T(8,128)(2,1)}, u32[]{:S(2)}) copy-start(bf16[256,16,32]{0,2,1:T(8,128)(2,1)} %get-tuple-element.330) | copy-start | bytes 786436
  133.4 50.4 %slice-start = ((s32[1,1024]{1,0:T(1,128)}), s32[1,512]{1,0:T(1,128)S(1)}, s32[]{:S(2)}) async-start(s32[1,1024]{1,0:T(1,128)} %param.20), calls=%async_computation.23 | async-start | bytes 4096 | tf_op jit(solution)/shard_map/slice | solution.py:55
  147.8 30.8 %all-to-all-start.2 = ((bf16[256,4,256]{0,2,1:T(8,128)(2,1)}), bf16[256,4,256]{0,2,1:T(8,128)(2,1)S(1)}, u32[]{:S(2)}, u32[]{:S(2)}) async-start(bf16[256,4,256]{0,2,1:T(8,128)(2,1)} %bitcast.39), calls=%async_computation.2 | async-start | bytes 1048576 | tf_op jit(solution)/shard_map/all_to_all | solution.py:196
  178.6 18.6 %all-to-all-start.1 = ((bf16[256,4,256]{0,2,1:T(8,128)(2,1)}), bf16[256,4,256]{0,2,1:T(8,128)(2,1)S(1)}, u32[]{:S(2)}, u32[]{:S(2)}) async-start(bf16[256,4,256]{0,2,1:T(8,128)(2,1)} %bitcast.36), calls=%async_computation.1 | async-start | bytes 1048576 | tf_op jit(solution)/shard_map/all_to_all | solution.py:195
  182.0 97.3 %all-reduce.14.cloned.1.call-start = ((), (), s32[]{:S(2)}) async-start(), calls=%async_computation.14 | async-start | bytes 2097152 | tf_op jit(solution)/shard_map/psum | solution.py:203
  202.7 2.5 copy-start.15
  209.8 2.5 copy-start.15
  214.7 26.2 %copy-start.7 = (bf16[2,512,256]{1,2,0:T(8,128)(2,1)}, bf16[2,512,256]{1,2,0:T(8,128)(2,1)S(1)}, u32[]{:S(2)}) copy-start(bf16[2,512,256]{1,2,0:T(8,128)(2,1)S(1)} %get-tuple-element.135) | copy-start | bytes 1572868
  240.9 1.2 copy-start.34
  240.9 217.7 %all-gather.11.cloned.1.call-start = ((), (), s32[]{:S(2)}) async-start(), calls=%async_computation.15 | async-start | bytes 35651584 | tf_op jit(solution)/shard_map/all_gather | solution.py:182
  241.5 349.0 %all-gather.13.cloned.1.call-start = ((), (), s32[]{:S(2)}) async-start(), calls=%async_computation.16 | async-start | bytes 17825792 | tf_op jit(solution)/shard_map/all_gather | solution.py:183
  242.1 416.9 %all-reduce.16.cloned.1.call-start = ((), (), s32[]{:S(2)}) async-start(), calls=%async_computation.17 | async-start | bytes 2097152 | tf_op jit(solution)/shard_map/psum | solution.py:229
  659.0 3.0 copy-start.2
  659.0 3.0 copy-start.4
  659.0 3.0 copy-start.6
  666.8 19.1 %all-to-all-start.4 = ((bf16[256,4,256]{0,2,1:T(8,128)(2,1)}), bf16[256,4,256]{0,2,1:T(8,128)(2,1)S(1)}, u32[]{:S(2)}, u32[]{:S(2)}) async-start(bf16[256,4,256]{0,2,1:T(8,128)(2,1)} %bitcast.280), calls=%async_computation.4 | async-start | bytes 1048576 | tf_op jit(solution)/shard_map/all_to_all | solution.py:241
  691.0 1.3 copy-start.8
  691.0 2.0 copy-start.16
  693.0 3.4 copy-start.21
  696.4 1.6 copy-start.11
  697.8 1.0 copy-start.22
  698.0 1.6 copy-start.13
  698.8 3.2 copy-start.12
  702.0 1.4 copy-start.14
  703.4 1.3 copy-start.8
  703.4 2.0 copy-start.16
  705.4 3.4 copy-start.21
  708.7 1.6 copy-start.11
  710.2 1.0 copy-start.22
  710.3 1.6 copy-start.13
  711.2 3.2 copy-start.12
  714.4 1.4 copy-start.14
  718.2 5.1 copy-start.23
  719.8 17.5 %all-to-all-start.7 = ((bf16[4,256,256]{1,2,0:T(8,128)(2,1)}), bf16[4,256,256]{1,2,0:T(8,128)(2,1)S(1)}, u32[]{:S(2)}, u32[]{:S(2)}) async-start(bf16[4,256,256]{1,2,0:T(8,128)(2,1)} %copy.98), calls=%async_computation.7 | async-start | bytes 1048576 | tf_op jit(solution)/shard_map/all_to_all | solution.py:250
  737.3 5.6 copy-start.10
  737.3 18.7 %all-to-all-start.5 = ((bf16[4,256,256]{1,2,0:T(8,128)(2,1)}), bf16[4,256,256]{1,2,0:T(8,128)(2,1)}, u32[]{:S(2)}, u32[]{:S(2)}) async-start(bf16[4,256,256]{1,2,0:T(8,128)(2,1)} %copy.94), calls=%async_computation.5 | async-start | bytes 1048576 | tf_op jit(solution)/shard_map/all_to_all | solution.py:248
  744.3 15.9 copy-start.9
  756.0 18.3 %all-to-all-start.6 = ((bf16[4,256,256]{1,2,0:T(8,128)(2,1)}), bf16[4,256,256]{1,2,0:T(8,128)(2,1)}, u32[]{:S(2)}, u32[]{:S(2)}) async-start(bf16[4,256,256]{1,2,0:T(8,128)(2,1)} %copy.96), calls=%async_computation.6 | async-start | bytes 1048576 | tf_op jit(solution)/shard_map/all_to_all | solution.py:249
  760.1 254.8 %all-reduce.18.cloned.1.call-start = ((), (), s32[]{:S(2)}) async-start(), calls=%async_computation.22 | async-start | bytes 4194304 | tf_op jit(solution)/shard_map/psum | solution.py:213
  769.4 6.0 copy-start.27
  769.4 6.0 copy-start.28
  770.7 5.6 copy-start.18
  776.0 0.8 copy-start.19
  776.8 0.8 copy-start.20
  786.6 1.2 copy-start.3
  786.6 1.5 copy-start.5
  786.6 269.8 %reduce-scatter.15.cloned.1.call-start = ((), (), s32[]{:S(2)}) async-start(), calls=%async_computation.19 | async-start | bytes 4456448
  799.5 0.7 copy-start.25
  799.5 0.7 copy-start.31
  799.5 264.0 %reduce-scatter.13.cloned.1.call-start = ((), (), s32[]{:S(2)}) async-start(), calls=%async_computation.18 | async-start | bytes 13369344
  851.6 392.5 %reduce-scatter.19.cloned.1.call-start = ((), (), s32[]{:S(2)}) async-start(), calls=%async_computation.21 | async-start | bytes 17825792
  883.5 694.7 %reduce-scatter.17.cloned.1.call-start = ((), (), s32[]{:S(2)}) async-start(), calls=%async_computation.20 | async-start | bytes 35651584
  1013.1 0.7 copy-start.35
  1013.1 3.8 copy-start.32
  1013.1 38.2 %copy-start.33 = (f32[256]{0:T(256)S(1)}, f32[256]{0:T(256)}, u32[]{:S(2)}) copy-start(f32[256]{0:T(256)} %get-tuple-element.334) | copy-start | bytes 3076
Sparse Core Ops, SparseCore 0:
  10.2 103.2 all-gather.6
  115.6 67.4 all-gather.8
  241.0 38.2 all-reduce.13
  280.7 177.8 all-gather.10
  460.5 129.8 all-gather.12
  620.7 38.2 all-reduce.15
  786.7 61.1 all-reduce.17
  851.7 72.7 reduce-scatter.14
  928.6 134.9 reduce-scatter.12
  1067.5 176.5 reduce-scatter.18
  1248.4 329.7 reduce-scatter.16
where the time goes:
time: 1610 us; the launch traced here: 1600 us
  waiting for transfers between devices  996 us (62%)
  local copies, waits for them, and re-layouts  256 us (16%)
  matrix products  148 us (9%)
  blocking collectives  116 us (7%)
  other arithmetic  37.1 us (2%)
  starting transfers between devices  29.3 us (2%)
    unnamed x15, waiting for transfers between devices  514 us
    unnamed x70, local copies, waits for them, and re-layouts  211 us
    all_gather x1, waiting for transfers between devices, on_device(): lax.all_gather(w_gate_up, ('shard', 'ctx'), axis=1, tiled=True)  178 us
    dot_general x24, matrix products, contract(): jnp.einsum(form, left_in, right_in, preferred_element_type=jnp.float32)  134 us
    all_gather x1, waiting for transfers between devices, on_device(): lax.all_gather(w_down, ('shard', 'ctx'), axis=1, tiled=True)  114 us
    all_gather x1, waiting for transfers between devices, on_device(): lax.all_gather(w_qkv, ('shard', 'ctx'), axis=1, tiled=True)  66.9 us
    psum x1, waiting for transfers between devices, on_device(): lax.psum(terms_two.astype(jnp.bfloat16), 'tp').astype(jnp.float32)  38.4 us
    all_gather x1, blocking collectives, on_device(): lax.all_gather(gain_attn, ('shard', 'ctx'), axis=0, tiled=True)  35 us
  transfers between devices with their start and end apart: 18, of which 15 were waited for; matrix products, arithmetic and copies ran while one was open for 21% of the time, Pallas kernels for 0%

commit v1 on v0

--- a/solution.py
+++ b/solution.py
@@ -7,6 +7,16 @@
 EPSILON = 1e-05
 ROPE_BASE = 130000.0
 MASKED = -1e30
+
+
+def knots_list(x0, out_dim):
+    x0 = jnp.moveaxis(x0, 0, out_dim)
+    all_values = x0.shape
+    return x0.reshape(
+        *all_values[:out_dim],
+        all_values[out_dim] * all_values[out_dim + 1],
+        *all_values[out_dim + 2 :]
+    )
 
 
 def contract(form, left_in, right_in):
@@ -168,6 +178,17 @@
 
 
 def on_device(hidden_in, gain_attn, w_qkv, w_out, gain_mlp, w_gate_up, w_down, segments, cotangent):
+
+    def lead_levels_all_by_axis(axis_name, d0, local_array):
+        world_n = lax.axis_size(axis_name)
+        views = tuple(((p, (p + 1) % world_n) for p in range(world_n)))
+        items = [local_array]
+        while len(items) < world_n:
+            items.append(lax.ppermute(items[-1], axis_name, views))
+        outcome_arr = lax.axis_index(axis_name)
+        items = jnp.stack(items)[(outcome_arr - jnp.arange(world_n)) % world_n]
+        return knots_list(items, d0)
+
     token_rows = hidden_in.shape[0]
     seg_row = segments[0]
     positions = lax.dynamic_slice_in_dim(
@@ -180,7 +201,7 @@
         lax.all_gather(w_out, ("shard", "ctx"), axis=1, tiled=True),
         lax.all_gather(gain_mlp, ("shard", "ctx"), axis=0, tiled=True),
         lax.all_gather(w_gate_up, ("shard", "ctx"), axis=1, tiled=True),
-        lax.all_gather(w_down, ("shard", "ctx"), axis=1, tiled=True),
+        lead_levels_all_by_axis(("shard", "ctx"), 1, w_down),
     )
     gain_full_one, qkv_full, out_full, gain_full_two, gate_up_full, down_full = gathered
     resid_in = hidden_in.astype(jnp.float32)

time: 1610 us -> 1900 us (1.18)
  waiting for transfers between devices: 996 us -> 1190 us
  local copies, waits for them, and re-layouts: 256 us -> 307 us
  blocking collectives: 116 us -> 145 us
    ppermute x0 -> x15, waiting for transfers between devices: none -> 365 us  [lead_levels_all_by_axis(): items.append(lax.ppermute(items[-1], axis_name, views))]
    all_gather x1, waiting for transfers between devices: 178 us -> 0.02 us  [on_device(): lax.all_gather(w_gate_up, ('shard', 'ctx'), axis=1, tiled=True)]
    all_gather x1, blocking collectives: 28.8 us -> 59.5 us  [on_device(): lax.all_gather(gain_mlp, ('shard', 'ctx'), axis=0, tiled=True)]
    unnamed x70 -> x81, local copies, waits for them, and re-layouts: 211 us -> 235 us
    transpose x0 -> x1, local copies, waits for them, and re-layouts: none -> 20.7 us  [knots_list(): x0 = jnp.moveaxis(x0, 0, out_dim)]
  transfers between devices with their start and end apart: 18 -> 33, of which waited for: 15 -> 22; matrix products, arithmetic and copies ran while one was open for 21% -> 25% of each run, Pallas kernels for 0% -> 0%
where the time goes in v1:
time: 1900 us; the launch traced here: 1890 us
  waiting for transfers between devices  1190 us (63%)
  local copies, waits for them, and re-layouts  307 us (16%)
  matrix products  163 us (9%)
  blocking collectives  145 us (8%)
  other arithmetic  34.5 us (2%)
  starting transfers between devices  34.4 us (2%)
    unnamed x15, waiting for transfers between devices  512 us
    ppermute x15, waiting for transfers between devices, lead_levels_all_by_axis(): items.append(lax.ppermute(items[-1], axis_name, views))  365 us
    unnamed x81, local copies, waits for them, and re-layouts  235 us
    dot_general x24, matrix products, contract(): jnp.einsum(form, left_in, right_in, preferred_element_type=jnp.float32)  139 us
    all_gather x1, waiting for transfers between devices, on_device(): lax.all_gather(w_down, ('shard', 'ctx'), axis=1, tiled=True)  121 us
    all_gather x1, waiting for transfers between devices, on_device(): lax.all_gather(w_qkv, ('shard', 'ctx'), axis=1, tiled=True)  66.2 us
    all_gather x1, blocking collectives, on_device(): lax.all_gather(gain_mlp, ('shard', 'ctx'), axis=0, tiled=True)  59.5 us
  transfers between devices with their start and end apart: 33, of which 22 were waited for; matrix products, arithmetic and copies ran while one was open for 25% of the time, Pallas kernels for 0%

profile of v1, /device:TPU:0, one launch (start us, length us, event | category | flops | bytes accessed | tf_op | source)
XLA Modules:
  0.0 1887.8 jit_solution(12613524223437182166)
XLA Ops:
  8.7 35.0 %all-gather = bf16[16,1,128]{2,1,0:T(2,128)(2,1)S(1)} all-gather(bf16[1,1,128]{2,1,0:T(2,128)(2,1)} %bitcast.372), channel_id=1, replica_groups=mesh['shard'=4,'ctx'=4,'tp'=2] {'shard','ctx'}, dimensions={0}, use_global_device_ids=true | all-gather | bytes 4352 | tf_op jit(solution)/shard_map/all_gather | solution.py:199
  47.4 66.2 %all-gather.7.cloned.1.call-done = bf16[3,2048,1024]{2,1,0:T(8,128)(2,1)} async-done(((bf16[3,128,1024]{2,1,0:T(8,128)(2,1)}), bf16[3,2048,1024]{2,1,0:T(8,128)(2,1)}) %all-gather.7.cloned.1.call-update) | async-done | bytes 12582928 | tf_op jit(solution)/shard_map/all_gather | solution.py:200
  113.5 6.9 convolution_bitcast_fusion.3
  123.3 4.2 all-to-all-start
  134.1 13.6 all-to-all-done
  147.8 3.5 all-to-all-start.2
  152.1 26.6 %all-to-all-done.2 = bf16[256,4,256]{0,2,1:T(8,128)(2,1)S(1)} async-done(((bf16[256,4,256]{0,2,1:T(8,128)(2,1)}), bf16[256,4,256]{0,2,1:T(8,128)(2,1)S(1)}, u32[]{:S(2)}, u32[]{:S(2)}) %all-to-all-start.2) | async-done | bytes 524320 | tf_op jit(solution)/shard_map/all_to_all | solution.py:217
  178.7 3.5 all-to-all-start.1
  190.9 6.4 all-to-all-done.1
  200.3 14.2 while.26
  214.8 16.7 all_to_all.107
  231.7 4.6 convolution_convert_fusion.3
  237.9 26.4 %collective-permute-done = bf16[4096,128]{1,0:T(8,128)(2,1)S(1)} collective-permute-done((bf16[4096,128]{1,0:T(8,128)(2,1)}, bf16[4096,128]{1,0:T(8,128)(2,1)S(1)}, u32[]{:S(2)}, u32[]{:S(2)}) %collective-permute-start) | collective-permute-done | bytes 1048608 | tf_op jit(solution)/shard_map/ppermute | solution.py:187
  264.3 27.6 %collective-permute-done.1 = bf16[4096,128]{1,0:T(8,128)(2,1)S(1)} collective-permute-done((bf16[4096,128]{1,0:T(8,128)(2,1)S(1)}, bf16[4096,128]{1,0:T(8,128)(2,1)S(1)}, u32[]{:S(2)}, u32[]{:S(2)}) %collective-permute-start.1) | collective-permute-done | bytes 1048608 | tf_op jit(solution)/shard_map/ppermute | solution.py:187
  291.9 37.1 %collective-permute-done.2 = bf16[4096,128]{1,0:T(8,128)(2,1)S(1)} collective-permute-done((bf16[4096,128]{1,0:T(8,128)(2,1)S(1)}, bf16[4096,128]{1,0:T(8,128)(2,1)S(1)}, u32[]{:S(2)}, u32[]{:S(2)}) %collective-permute-start.2) | collective-permute-done | bytes 1048608 | tf_op jit(solution)/shard_map/ppermute | solution.py:187
  329.9 36.9 %collective-permute-done.3 = bf16[4096,128]{1,0:T(8,128)(2,1)S(1)} collective-permute-done((bf16[4096,128]{1,0:T(8,128)(2,1)S(1)}, bf16[4096,128]{1,0:T(8,128)(2,1)S(1)}, u32[]{:S(2)}, u32[]{:S(2)}) %collective-permute-start.3) | collective-permute-done | bytes 1048608 | tf_op jit(solution)/shard_map/ppermute | solution.py:187
  367.8 35.6 %collective-permute-done.4 = bf16[4096,128]{1,0:T(8,128)(2,1)} collective-permute-done((bf16[4096,128]{1,0:T(8,128)(2,1)S(1)}, bf16[4096,128]{1,0:T(8,128)(2,1)}, u32[]{:S(2)}, u32[]{:S(2)}) %collective-permute-start.4) | collective-permute-done | bytes 1048608 | tf_op jit(solution)/shard_map/ppermute | solution.py:187
  403.4 59.5 %all-gather.1 = bf16[16,1,128]{2,1,0:T(2,128)(2,1)S(1)} all-gather(bf16[1,1,128]{2,1,0:T(2,128)(2,1)S(1)} %bitcast.373), channel_id=1, replica_groups=mesh['shard'=4,'ctx'=4,'tp'=2] {'shard','ctx'}, dimensions={0}, use_global_device_ids=true | all-gather | bytes 4352 | tf_op jit(solution)/shard_map/all_gather | solution.py:202
  467.6 33.9 %collective-permute-done.6 = bf16[4096,128]{1,0:T(8,128)(2,1)S(1)} collective-permute-done((bf16[4096,128]{1,0:T(8,128)(2,1)}, bf16[4096,128]{1,0:T(8,128)(2,1)S(1)}, u32[]{:S(2)}, u32[]{:S(2)}) %collective-permute-start.6) | collective-permute-done | bytes 1048608 | tf_op jit(solution)/shard_map/ppermute | solution.py:187
  503.6 36.0 %collective-permute-done.7 = bf16[4096,128]{1,0:T(8,128)(2,1)S(1)} collective-permute-done((bf16[4096,128]{1,0:T(8,128)(2,1)S(1)}, bf16[4096,128]{1,0:T(8,128)(2,1)S(1)}, u32[]{:S(2)}, u32[]{:S(2)}) %collective-permute-start.7) | collective-permute-done | bytes 1048608 | tf_op jit(solution)/shard_map/ppermute | solution.py:187
  541.7 35.7 %collective-permute-done.8 = bf16[4096,128]{1,0:T(8,128)(2,1)S(1)} collective-permute-done((bf16[4096,128]{1,0:T(8,128)(2,1)S(1)}, bf16[4096,128]{1,0:T(8,128)(2,1)S(1)}, u32[]{:S(2)}, u32[]{:S(2)}) %collective-permute-start.8) | collective-permute-done | bytes 1048608 | tf_op jit(solution)/shard_map/ppermute | solution.py:187
  582.0 32.9 %collective-permute-done.9 = bf16[4096,128]{1,0:T(8,128)(2,1)S(1)} collective-permute-done((bf16[4096,128]{1,0:T(8,128)(2,1)S(1)}, bf16[4096,128]{1,0:T(8,128)(2,1)S(1)}, u32[]{:S(2)}, u32[]{:S(2)}) %collective-permute-start.9) | collective-permute-done | bytes 1048608 | tf_op jit(solution)/shard_map/ppermute | solution.py:187
  617.2 35.1 %collective-permute-done.10 = bf16[4096,128]{1,0:T(8,128)(2,1)S(1)} collective-permute-done((bf16[4096,128]{1,0:T(8,128)(2,1)S(1)}, bf16[4096,128]{1,0:T(8,128)(2,1)S(1)}, u32[]{:S(2)}, u32[]{:S(2)}) %collective-permute-start.10) | collective-permute-done | bytes 1048608 | tf_op jit(solution)/shard_map/ppermute | solution.py:187
  655.4 28.2 %collective-permute-done.11 = bf16[4096,128]{1,0:T(8,128)(2,1)} collective-permute-done((bf16[4096,128]{1,0:T(8,128)(2,1)S(1)}, bf16[4096,128]{1,0:T(8,128)(2,1)}, u32[]{:S(2)}, u32[]{:S(2)}) %collective-permute-start.11) | collective-permute-done | bytes 1048608 | tf_op jit(solution)/shard_map/ppermute | solution.py:187
  685.4 17.4 convolution_bitcast_fusion
  702.8 120.8 %all-gather.13.cloned.1.call-done = bf16[4096,2048]{1,0:T(8,128)(2,1)} async-done(((bf16[4096,128]{1,0:T(8,128)(2,1)}), bf16[4096,2048]{1,0:T(8,128)(2,1)}) %all-gather.13.cloned.1.call-update) | async-done | bytes 16777232 | tf_op jit(solution)/shard_map/all_gather | solution.py:240
  823.6 12.9 fusion.88
  836.5 16.7 fusion.63
  857.8 33.8 %all-reduce.16.cloned.1.call-done = bf16[256,2048]{1,0:T(8,128)(2,1)} async-done(((bf16[256,2048]{1,0:T(8,128)(2,1)}), bf16[256,2048]{1,0:T(8,128)(2,1)}) %all-reduce.16.cloned.1.call-update) | async-done | bytes 1048592 | tf_op jit(solution)/shard_map/psum | solution.py:250
  891.6 2.9 fusion.74
  894.5 4.8 convolution_convert_fusion.4
  900.2 4.6 all-to-all-start.4
  909.3 32.3 %all-to-all-done.4 = bf16[256,4,256]{0,2,1:T(8,128)(2,1)S(1)} async-done(((bf16[256,4,256]{0,2,1:T(8,128)(2,1)}), bf16[256,4,256]{0,2,1:T(8,128)(2,1)S(1)}, u32[]{:S(2)}, u32[]{:S(2)}) %all-to-all-start.4) | async-done | bytes 524320 | tf_op jit(solution)/shard_map/all_to_all | solution.py:262
  942.8 2.6 reshape_reshape.18
  946.6 24.8 %while.27 = (s32[]{:T(128)}, bf16[2,512,4,64]{1,3,2,0:T(8,128)(2,1)}, f32[2,1024,4,64]{1,3,2,0:T(8,128)}, f32[2,1024,4,64]{1,3,2,0:T(8,128)}, bf16[2,1024,4,64]{...) while((s32[]{:T(128)}, ...), condition=%wide.region_14.15_spmd, body=%wide.region_12.14_spmd.sunk | while | flops 1365637120 | bytes 89220488 | solution.py:151
  948.6 3.3 multiply_convert_fusion.5
  961.0 3.3 multiply_convert_fusion.5
  975.5 3.5 all-to-all-start.7
  982.8 10.1 all-to-all-done.7
  992.9 3.9 all-to-all-start.5
  999.1 13.1 gather_fusion
  1012.2 20.7 %copy.90 = bf16[4096,16,128]{0,2,1:T(8,128)(2,1)} copy(bf16[4096,16,128]{2,0,1:T(8,128)(2,1)} %bitcast.326) | data formatting | bytes 33554432 | tf_op jit(solution)/shard_map/transpose | solution.py:13
  1036.9 5.1 all-to-all-start.6
  1042.0 19.1 %convolution_convert_fusion.2 = bf16[256,2048]{1,0:T(8,128)(2,1)} fusion(bf16[4096,2048]{0,1:T(8,128)(2,1)} %bitcast.328, f32[2,256,4096]{2,1,0:T(8,128)} %convolution_bitcast_fusion), kind=kOutput, calls=%fused_computation.105 | convolution fusion | flops 4301783040 | bytes 26214400 | tf_op jit(solution)/shard_map/dot_general | solution.py:232
  1064.8 9.6 fusion.64
  1074.6 5.0 convolution_convert_fusion.1
  1079.6 6.6 copy.115
  1086.9 8.0 convert_bitcast_fusion.1
  1094.9 27.7 %copy.113 = bf16[3,2048,1024]{2,0,1:T(4,128)(2,1)} copy(bf16[3,2048,1024]{1,2,0:T(8,128)(2,1)} %convert_bitcast_fusion.1) | data formatting | bytes 25165824
  1122.6 15.9 copy.121
  1138.5 14.9 convolution_convert_fusion
  1153.4 21.7 %copy.119 = bf16[4096,2048]{0,1:T(8,128)(2,1)} copy(bf16[4096,2048]{1,0:T(8,128)(2,1)} %convolution_convert_fusion) | data formatting | bytes 33554432
  1175.4 16.4 convert_bitcast_fusion
  1191.8 83.2 %copy.117 = bf16[2,2048,4096]{2,0,1:T(2,128)(2,1)} copy(bf16[2,2048,4096]{1,2,0:T(8,128)(2,1)} %convert_bitcast_fusion) | data formatting | bytes 67108864
  1275.0 29.5 %copy.122 = bf16[256,8,2,4096]{3,1,2,0:T(8,128)(2,1)} copy(bf16[256,8,2,4096]{3,2,1,0:T(2,128)(2,1)} %bitcast.323) | data formatting | bytes 67108864
  1308.3 34.2 %all-reduce.8 = (bf16[2048]{0:T(1024)(128)(2,1)S(1)}, bf16[2048]{0:T(1024)(128)(2,1)S(1)}) all-reduce(bf16[2048]{0:T(1024)(128)(2,1)S(1)} %get-tuple-element.246, bf16[2048]{0:T(1024)(128)(2,1)S(1)} %copy-done.30), channel_id=2, replica_groups=mesh['shard'=4,'ctx'=4,'tp'=2] {'shard','ctx'}, use_global_device_ids=true, to_apply=%region_18.19.clone | all-reduce | flops 4096 | bytes 16384
  1343.7 5.1 fusion.69
  1350.8 3.4 reduce-scatter.13.cloned.1.call-done
  1354.2 2.7 reshape.486
  1359.2 175.2 %reduce-scatter.19.cloned.1.call-done = bf16[128,4096]{1,0:T(8,128)(2,1)} async-done(((bf16[2048,4096]{1,0:T(8,128)(2,1)}), bf16[128,4096]{1,0:T(8,128)(2,1)}) %reduce-scatter.19.cloned.1.call-update) | async-done | bytes 1048592
  1537.5 330.9 %reduce-scatter.17.cloned.1.call-done = bf16[128,8192]{1,0:T(8,128)(2,1)} async-done(((bf16[2048,8192]{1,0:T(8,128)(2,1)}), bf16[128,8192]{1,0:T(8,128)(2,1)}) %reduce-scatter.17.cloned.1.call-update) | async-done | bytes 2097168
  1868.5 4.5 reshape.490
  1872.9 4.9 copy.118
  1877.8 3.2 copy.107
  (277 shorter events, 126.4 us)
Async XLA Ops:
  7.2 106.3 %all-gather.7.cloned.1.call-start = ((), (), s32[]{:S(2)}) async-start(), calls=%async_computation.12 | async-start | bytes 13369344 | tf_op jit(solution)/shard_map/all_gather | solution.py:200
  7.9 223.8 %all-gather.9.cloned.1.call-start = ((), (), s32[]{:S(2)}) async-start(), calls=%async_computation.13 | async-start | bytes 4456448 | tf_op jit(solution)/shard_map/all_gather | solution.py:201
  43.6 76.7 %copy-start.22 = (f32[16,1,128]{2,1,0:T(1,128)}, f32[16,1,128]{2,1,0:T(1,128)S(1)}, u32[]{:S(2)}) copy-start(f32[16,1,128]{2,1,0:T(1,128)S(1)} %convert_element_type.264) | copy-start | bytes 24580
  45.8 74.6 %copy-start.28 = (f32[256]{0:T(256)}, f32[256]{0:T(256)S(1)}, u32[]{:S(2)}) copy-start(f32[256]{0:T(256)S(1)} %get-tuple-element.334) | copy-start | bytes 3076
  123.3 24.4 %all-to-all-start = ((bf16[256,4,256]{0,2,1:T(8,128)(2,1)}), bf16[256,4,256]{0,2,1:T(8,128)(2,1)}, u32[]{:S(2)}, u32[]{:S(2)}) async-start(bf16[256,4,256]{0,2,1:T(8,128)(2,1)} %bitcast.344), calls=%async_computation | async-start | bytes 1048576 | tf_op jit(solution)/shard_map/all_to_all | solution.py:218
  128.3 4.7 copy-start.24
  132.9 50.3 %copy-start.27 = (s32[1,1024]{1,0:T(1,128)S(1)}, s32[1,1024]{1,0:T(1,128)}, u32[]{:S(2)}) copy-start(s32[1,1024]{1,0:T(1,128)} %param.20) | copy-start | bytes 12292
  133.0 51.0 %slice-start = ((s32[1,1024]{1,0:T(1,128)}), s32[1,512]{1,0:T(1,128)S(1)}, s32[]{:S(2)}) async-start(s32[1,1024]{1,0:T(1,128)} %param.20), calls=%async_computation.23 | async-start | bytes 4096 | tf_op jit(solution)/shard_map/slice | solution.py:65
  147.8 30.9 %all-to-all-start.2 = ((bf16[256,4,256]{0,2,1:T(8,128)(2,1)}), bf16[256,4,256]{0,2,1:T(8,128)(2,1)S(1)}, u32[]{:S(2)}, u32[]{:S(2)}) async-start(bf16[256,4,256]{0,2,1:T(8,128)(2,1)} %bitcast.39), calls=%async_computation.2 | async-start | bytes 1048576 | tf_op jit(solution)/shard_map/all_to_all | solution.py:217
  178.7 18.6 all-to-all-start.1
  182.2 501.4 %all-reduce.14.cloned.1.call-start = ((), (), s32[]{:S(2)}) async-start(), calls=%async_computation.14 | async-start | bytes 2097152 | tf_op jit(solution)/shard_map/psum | solution.py:224
  202.6 2.5 copy-start.10
  209.7 2.5 copy-start.10
  214.5 21.8 %copy-start.3 = (bf16[2,512,256]{1,2,0:T(8,128)(2,1)}, bf16[2,512,256]{1,2,0:T(8,128)(2,1)S(1)}, u32[]{:S(2)}) copy-start(bf16[2,512,256]{1,2,0:T(8,128)(2,1)S(1)} %get-tuple-element.135) | copy-start | bytes 1572868
  231.7 5.3 copy-start.5
  231.7 171.7 %copy-start.32 = (bf16[128]{0:T(256)(128)(2,1)S(1)}, bf16[128]{0:T(256)(128)(2,1)}, u32[]{:S(2)}) copy-start(bf16[128]{0:T(256)(128)(2,1)} %param.17) | copy-start | bytes 772
  236.4 449.0 %all-gather.11.cloned.1.call-start = ((), (), s32[]{:S(2)}) async-start(), calls=%async_computation.15 | async-start | bytes 35651584 | tf_op jit(solution)/shard_map/all_gather | solution.py:203
  237.0 586.6 %all-gather.13.cloned.1.call-start = ((), (), s32[]{:S(2)}) async-start(), calls=%async_computation.16 | async-start | bytes 17825792 | tf_op jit(solution)/shard_map/all_gather | solution.py:240
  237.5 654.1 %all-reduce.16.cloned.1.call-start = ((), (), s32[]{:S(2)}) async-start(), calls=%async_computation.17 | async-start | bytes 2097152 | tf_op jit(solution)/shard_map/psum | solution.py:250
  237.6 26.7 %collective-permute-start = (bf16[4096,128]{1,0:T(8,128)(2,1)}, bf16[4096,128]{1,0:T(8,128)(2,1)S(1)}, u32[]{:S(2)}, u32[]{:S(2)}) collective-permute-start(bf16[4096,128]{1,0:T(8,128)(2,1)} %param.19), channel_id=1, source_target_pairs={{0,2},{2,4},{4,6},{6,8},{8,10},{10,12},{12,14},{14,16},{16,18},{18... | collective-permute-start | bytes 3145736 | tf_op jit(solution)/shard_map/ppermute | solution.py:187
  264.3 27.6 %collective-permute-start.1 = (bf16[4096,128]{1,0:T(8,128)(2,1)S(1)}, bf16[4096,128]{1,0:T(8,128)(2,1)S(1)}, u32[]{:S(2)}, u32[]{:S(2)}) collective-permute-start(bf16[4096,128]{1,0:T(8,128)(2,1)S(1)} %collective-permute-done), channel_id=1, source_target_pairs={{0,2},{2,4},{4,6},{6,8},{8,10},{10,12},{12,14},{14,16},{16,18},{18... | collective-permute-start | bytes 3145736 | tf_op jit(solution)/shard_map/ppermute | solution.py:187
  291.9 74.9 %copy-start.14 = (bf16[4096,128]{1,0:T(8,128)(2,1)}, bf16[4096,128]{1,0:T(8,128)(2,1)S(1)}, u32[]{:S(2)}) copy-start(bf16[4096,128]{1,0:T(8,128)(2,1)S(1)} %collective-permute-done.1) | copy-start | bytes 3145732
  291.9 37.1 %collective-permute-start.2 = (bf16[4096,128]{1,0:T(8,128)(2,1)S(1)}, bf16[4096,128]{1,0:T(8,128)(2,1)S(1)}, u32[]{:S(2)}, u32[]{:S(2)}) collective-permute-start(bf16[4096,128]{1,0:T(8,128)(2,1)S(1)} %collective-permute-done.1), channel_id=1, source_target_pairs={{0,2},{2,4},{4,6},{6,8},{8,10},{10,12},{12,14},{14,16},{16,18},{18... | collective-permute-start | bytes 3145736 | tf_op jit(solution)/shard_map/ppermute | solution.py:187
  329.9 36.9 %collective-permute-start.3 = (bf16[4096,128]{1,0:T(8,128)(2,1)S(1)}, bf16[4096,128]{1,0:T(8,128)(2,1)S(1)}, u32[]{:S(2)}, u32[]{:S(2)}) collective-permute-start(bf16[4096,128]{1,0:T(8,128)(2,1)S(1)} %collective-permute-done.2), channel_id=1, source_target_pairs={{0,2},{2,4},{4,6},{6,8},{8,10},{10,12},{12,14},{14,16},{16,18},{18... | collective-permute-start | bytes 3145736 | tf_op jit(solution)/shard_map/ppermute | solution.py:187
  366.8 36.6 %collective-permute-start.4 = (bf16[4096,128]{1,0:T(8,128)(2,1)S(1)}, bf16[4096,128]{1,0:T(8,128)(2,1)}, u32[]{:S(2)}, u32[]{:S(2)}) collective-permute-start(bf16[4096,128]{1,0:T(8,128)(2,1)S(1)} %collective-permute-done.3), channel_id=1, source_target_pairs={{0,2},{2,4},{4,6},{6,8},{8,10},{10,12},{12,14},{14,16},{16,18},{18... | collective-permute-start | bytes 3145736 | tf_op jit(solution)/shard_map/ppermute | solution.py:187
  403.4 59.5 %collective-permute-start.5 = (bf16[4096,128]{1,0:T(8,128)(2,1)}, bf16[4096,128]{1,0:T(8,128)(2,1)}, u32[]{:S(2)}, u32[]{:S(2)}) collective-permute-start(bf16[4096,128]{1,0:T(8,128)(2,1)} %collective-permute-done.4), channel_id=1, source_target_pairs={{0,2},{2,4},{4,6},{6,8},{8,10},{10,12},{12,14},{14,16},{16,18},{18... | collective-permute-start | bytes 3145736 | tf_op jit(solution)/shard_map/ppermute | solution.py:187
  403.4 99.2 %copy-start.15 = (bf16[4096,128]{1,0:T(8,128)(2,1)S(1)}, bf16[4096,128]{1,0:T(8,128)(2,1)}, u32[]{:S(2)}) copy-start(bf16[4096,128]{1,0:T(8,128)(2,1)} %copy-done.14) | copy-start | bytes 3145732
  403.4 136.2 %copy-start.13 = (bf16[4096,128]{1,0:T(8,128)(2,1)S(1)}, bf16[4096,128]{1,0:T(8,128)(2,1)}, u32[]{:S(2)}) copy-start(bf16[4096,128]{1,0:T(8,128)(2,1)} %copy-done.12) | copy-start | bytes 3145732
  462.9 38.6 %collective-permute-start.6 = (bf16[4096,128]{1,0:T(8,128)(2,1)}, bf16[4096,128]{1,0:T(8,128)(2,1)S(1)}, u32[]{:S(2)}, u32[]{:S(2)}) collective-permute-start(bf16[4096,128]{1,0:T(8,128)(2,1)} %collective-permute-done.5), channel_id=1, source_target_pairs={{0,2},{2,4},{4,6},{6,8},{8,10},{10,12},{12,14},{14,16},{16,18},{18... | collective-permute-start | bytes 3145736 | tf_op jit(solution)/shard_map/ppermute | solution.py:187
  465.2 75.4 %copy-start.17 = (bf16[4096,128]{1,0:T(8,128)(2,1)S(1)}, bf16[4096,128]{1,0:T(8,128)(2,1)}, u32[]{:S(2)}) copy-start(bf16[4096,128]{1,0:T(8,128)(2,1)} %copy-done.16) | copy-start | bytes 3145732
  501.5 38.1 %collective-permute-start.7 = (bf16[4096,128]{1,0:T(8,128)(2,1)S(1)}, bf16[4096,128]{1,0:T(8,128)(2,1)S(1)}, u32[]{:S(2)}, u32[]{:S(2)}) collective-permute-start(bf16[4096,128]{1,0:T(8,128)(2,1)S(1)} %collective-permute-done.6), channel_id=1, source_target_pairs={{0,2},{2,4},{4,6},{6,8},{8,10},{10,12},{12,14},{14,16},{16,18},{18... | collective-permute-start | bytes 3145736 | tf_op jit(solution)/shard_map/ppermute | solution.py:187
  539.6 37.8 %collective-permute-start.8 = (bf16[4096,128]{1,0:T(8,128)(2,1)S(1)}, bf16[4096,128]{1,0:T(8,128)(2,1)S(1)}, u32[]{:S(2)}, u32[]{:S(2)}) collective-permute-start(bf16[4096,128]{1,0:T(8,128)(2,1)S(1)} %collective-permute-done.7), channel_id=1, source_target_pairs={{0,2},{2,4},{4,6},{6,8},{8,10},{10,12},{12,14},{14,16},{16,18},{18... | collective-permute-start | bytes 3145736 | tf_op jit(solution)/shard_map/ppermute | solution.py:187
  577.4 37.5 %collective-permute-start.9 = (bf16[4096,128]{1,0:T(8,128)(2,1)S(1)}, bf16[4096,128]{1,0:T(8,128)(2,1)S(1)}, u32[]{:S(2)}, u32[]{:S(2)}) collective-permute-start(bf16[4096,128]{1,0:T(8,128)(2,1)S(1)} %collective-permute-done.8), channel_id=1, source_target_pairs={{0,2},{2,4},{4,6},{6,8},{8,10},{10,12},{12,14},{14,16},{16,18},{18... | collective-permute-start | bytes 3145736 | tf_op jit(solution)/shard_map/ppermute | solution.py:187
  582.0 101.6 %copy-start = (bf16[256,2048]{1,0:T(8,128)(2,1)S(1)}, bf16[256,2048]{1,0:T(8,128)(2,1)}, u32[]{:S(2)}) copy-start(bf16[256,2048]{1,0:T(8,128)(2,1)} %param.13) | copy-start | bytes 3145732
  614.9 37.4 %collective-permute-start.10 = (bf16[4096,128]{1,0:T(8,128)(2,1)S(1)}, bf16[4096,128]{1,0:T(8,128)(2,1)S(1)}, u32[]{:S(2)}, u32[]{:S(2)}) collective-permute-start(bf16[4096,128]{1,0:T(8,128)(2,1)S(1)} %collective-permute-done.9), channel_id=1, source_target_pairs={{0,2},{2,4},{4,6},{6,8},{8,10},{10,12},{12,14},{14,16},{16,18},{18... | collective-permute-start | bytes 3145736 | tf_op jit(solution)/shard_map/ppermute | solution.py:187
  653.3 30.3 %collective-permute-start.11 = (bf16[4096,128]{1,0:T(8,128)(2,1)S(1)}, bf16[4096,128]{1,0:T(8,128)(2,1)}, u32[]{:S(2)}, u32[]{:S(2)}) collective-permute-start(bf16[4096,128]{1,0:T(8,128)(2,1)S(1)} %collective-permute-done.10), channel_id=1, source_target_pairs={{0,2},{2,4},{4,6},{6,8},{8,10},{10,12},{12,14},{14,16},{16,18},{18... | collective-permute-start | bytes 3145736 | tf_op jit(solution)/shard_map/ppermute | solution.py:187
  683.6 174.2 %collective-permute-start.12 = (bf16[4096,128]{1,0:T(8,128)(2,1)}, bf16[4096,128]{1,0:T(8,128)(2,1)}, u32[]{:S(2)}, u32[]{:S(2)}) collective-permute-start(bf16[4096,128]{1,0:T(8,128)(2,1)} %collective-permute-done.11), channel_id=1, source_target_pairs={{0,2},{2,4},{4,6},{6,8},{8,10},{10,12},{12,14},{14,16},{16,18},{18... | collective-permute-start | bytes 3145736 | tf_op jit(solution)/shard_map/ppermute | solution.py:187
  857.8 49.3 %collective-permute-start.13 = (bf16[4096,128]{1,0:T(8,128)(2,1)}, bf16[4096,128]{1,0:T(8,128)(2,1)}, u32[]{:S(2)}, u32[]{:S(2)}) collective-permute-start(bf16[4096,128]{1,0:T(8,128)(2,1)} %collective-permute-done.12), channel_id=1, source_target_pairs={{0,2},{2,4},{4,6},{6,8},{8,10},{10,12},{12,14},{14,16},{16,18},{18... | collective-permute-start | bytes 3145736 | tf_op jit(solution)/shard_map/ppermute | solution.py:187
  900.2 41.4 %all-to-all-start.4 = ((bf16[256,4,256]{0,2,1:T(8,128)(2,1)}), bf16[256,4,256]{0,2,1:T(8,128)(2,1)S(1)}, u32[]{:S(2)}, u32[]{:S(2)}) async-start(bf16[256,4,256]{0,2,1:T(8,128)(2,1)} %bitcast.346), calls=%async_computation.4 | async-start | bytes 1048576 | tf_op jit(solution)/shard_map/all_to_all | solution.py:262
  907.1 89.7 %collective-permute-start.14 = (bf16[4096,128]{1,0:T(8,128)(2,1)}, bf16[4096,128]{1,0:T(8,128)(2,1)}, u32[]{:S(2)}, u32[]{:S(2)}) collective-permute-start(bf16[4096,128]{1,0:T(8,128)(2,1)} %collective-permute-done.13), channel_id=1, source_target_pairs={{0,2},{2,4},{4,6},{6,8},{8,10},{10,12},{12,14},{14,16},{16,18},{18... | collective-permute-start | bytes 3145736 | tf_op jit(solution)/shard_map/ppermute | solution.py:187
  946.6 2.0 copy-start.11
  948.6 3.4 copy-start.19
  952.0 1.6 copy-start.6
  953.4 4.2 copy-start.20
  953.4 1.8 copy-start.8
  954.4 3.2 copy-start.7
  959.0 2.0 copy-start.11
  961.0 3.4 copy-start.19
  965.8 4.2 copy-start.20
  965.8 1.8 copy-start.8
  966.8 3.2 copy-start.7
  972.4 8.8 copy-start.21
  975.5 17.5 all-to-all-start.7
  992.9 44.0 %all-to-all-start.5 = ((bf16[4,256,256]{1,2,0:T(8,128)(2,1)}), bf16[4,256,256]{1,2,0:T(8,128)(2,1)S(1)}, u32[]{:S(2)}, u32[]{:S(2)}) async-start(bf16[4,256,256]{1,2,0:T(8,128)(2,1)} %copy.96), calls=%async_computation.5 | async-start | bytes 1048576 | tf_op jit(solution)/shard_map/all_to_all | solution.py:269
  1036.9 25.3 %all-to-all-start.6 = ((bf16[4,256,256]{1,2,0:T(8,128)(2,1)}), bf16[4,256,256]{1,2,0:T(8,128)(2,1)S(1)}, u32[]{:S(2)}, u32[]{:S(2)}) async-start(bf16[4,256,256]{1,2,0:T(8,128)(2,1)} %copy.98), calls=%async_computation.6 | async-start | bytes 1048576 | tf_op jit(solution)/shard_map/all_to_all | solution.py:270
  1042.0 264.5 %all-reduce.18.cloned.1.call-start = ((), (), s32[]{:S(2)}) async-start(), calls=%async_computation.22 | async-start | bytes 4194304 | tf_op jit(solution)/shard_map/psum | solution.py:234
  1064.8 9.9 copy-start.1
  1064.8 9.9 copy-start.2
  1074.4 274.5 %reduce-scatter.15.cloned.1.call-start = ((), (), s32[]{:S(2)}) async-start(), calls=%async_computation.19 | async-start | bytes 4456448
  1086.2 268.0 %reduce-scatter.13.cloned.1.call-start = ((), (), s32[]{:S(2)}) async-start(), calls=%async_computation.18 | async-start | bytes 13369344
  1138.5 396.0 %reduce-scatter.19.cloned.1.call-start = ((), (), s32[]{:S(2)}) async-start(), calls=%async_computation.21 | async-start | bytes 17825792
  1175.1 693.3 %reduce-scatter.17.cloned.1.call-start = ((), (), s32[]{:S(2)}) async-start(), calls=%async_computation.20 | async-start | bytes 35651584
  1304.5 3.8 copy-start.30
  1304.5 39.2 %copy-start.31 = (f32[256]{0:T(256)S(1)}, f32[256]{0:T(256)}, u32[]{:S(2)}) copy-start(f32[256]{0:T(256)} %get-tuple-element.333) | copy-start | bytes 3076
  (13 other events, 14.2 us)
Sparse Core Ops, SparseCore 0:
  10.2 103.2 all-gather.6
  115.6 67.7 all-gather.8
  236.5 38.6 all-reduce.13
  276.6 397.7 all-gather.10
  676.3 147.2 all-gather.12
  853.3 38.2 all-reduce.15
  1074.5 63.4 all-reduce.17
  1141.9 72.8 reduce-scatter.14
  1218.8 135.3 reduce-scatter.12
  1358.2 176.2 reduce-scatter.18
  1538.7 329.7 reduce-scatter.16
